TPU v7x, 32 devices: a whole 2x2x4 slice. The times are simulated.
32 devices in a mesh: seq: 16 (over z, y, x), mp: 2 (over core).
Axes of the slice: x: 2, y: 2, z: 4, core: 2. Of those that a mesh axis runs over, the one named last changes fastest.
Arguments:
- layer_input: bfloat16 [128, 8192], P('seq'), may hold values from -6 to 6
- w_query: bfloat16 [8192, 8192], P('seq', 'mp'), may hold values from -0.0625 to 0.0625
- w_key: bfloat16 [8192, 1024], P('seq', 'mp'), may hold values from -0.1875 to 0.1875
- w_value: bfloat16 [8192, 1024], P('seq', 'mp'), may hold values from -0.0625 to 0.0625
- w_out: bfloat16 [8192, 8192], P('mp', 'seq'), may hold values from -0.0625 to 0.0625
- kv_cache: bfloat16 [2, 32, 4096, 1024], P(None, None, 'seq', 'mp'), may hold values from -180 to 180, as said below
- cache_len: int32 [32], replicated, may hold values from 1 to 4096, as said below
Outputs:
- attn_out: bfloat16 [128, 8192], P('mp', 'seq')
Inputs may be any that keep to these rules, and one draw needn't show every extreme that they name: kv_cache entries at positions at or beyond a request's cache_len are never read. `cache_len`: exactly 4096 for at least one request.
All inputs are finite; a program needn't handle non-finite values.
Results may differ from a plain program's by a relative error of at most 0.012.
The roundings to bfloat16 on the way count: a program that leaves them out, or rounds other values in their place, can miss the bound.
Values may be sent and summed in bfloat16 or wider, within the bound.
A program may use at most 192 MiB of HBM per device.

v0:
```python
import math

import jax
import jax.numpy as jnp
from jax import lax
from jax.sharding import PartitionSpec as P

HD = 128


NEG_FILL = -1e30


def inverse_freq():
    index = jnp.arange(HD // 2, dtype=jnp.float32)
    base_freq = jnp.exp(-(2.0 * index / HD) * math.log(500000.0))
    wavelength = 2.0 * math.pi / base_freq
    smooth = jnp.clip((8192.0 / wavelength - 1.0) / 3.0, 0.0, 1.0)
    return (1.0 - smooth) * base_freq / 8.0 + smooth * base_freq


def rotate(values, positions):
    angles = positions.astype(jnp.float32)[..., None] * inverse_freq()
    cosine = jnp.cos(angles)
    sines = jnp.sin(angles)
    half_width = HD // 2
    first_half = values[..., :half_width]
    second_half = values[..., half_width:]
    return jnp.concatenate(
        [first_half * cosine - second_half * sines, second_half * cosine + first_half * sines],
        axis=-1,
    )


def shards(layer_input, w_query, w_key, w_value, w_out, kv_cache, cache_len):
    widened = layer_input.astype(jnp.float32)
    normed = (
        widened * lax.rsqrt(jnp.mean(widened * widened, axis=-1, keepdims=True) + 1e-05)
    ).astype(jnp.bfloat16)
    gathered = lax.all_to_all(normed, "seq", split_axis=1, concat_axis=0, tiled=True)
    partial_query = jnp.dot(gathered, w_query, preferred_element_type=jnp.float32)
    partial_key = jnp.dot(gathered, w_key, preferred_element_type=jnp.float32)
    partial_value = jnp.dot(gathered, w_value, preferred_element_type=jnp.float32)
    row_count = gathered.shape[0]
    request_count = cache_len.shape[0]
    decode_count = row_count // request_count
    heads_here = partial_query.shape[1] // HD
    kv_here = partial_key.shape[1] // HD
    group_size = heads_here // kv_here
    score_scale = 1.0 / math.sqrt(HD)
    highest = lax.Precision.HIGHEST
    query_all, key_all, value_all = lax.psum((partial_query, partial_key, partial_value), "seq")
    positions = (cache_len[:, None] + jnp.arange(decode_count, dtype=jnp.int32)[None, :]).reshape(
        row_count
    )
    queries = rotate(query_all.reshape(row_count, heads_here, HD), positions[:, None]).astype(
        jnp.bfloat16
    )
    keys_new = rotate(key_all.reshape(row_count, kv_here, HD), positions[:, None]).astype(
        jnp.bfloat16
    )
    values_new = value_all.astype(jnp.bfloat16)
    queries = queries.reshape(request_count, decode_count, kv_here, group_size, HD)
    keys_new = keys_new.reshape(request_count, decode_count, kv_here, HD)
    values_new = values_new.reshape(request_count, decode_count, kv_here, HD)
    block_size = kv_cache.shape[2]
    cache_keys = kv_cache[0].reshape(request_count, block_size, kv_here, HD)
    cache_values = kv_cache[1].reshape(request_count, block_size, kv_here, HD).astype(jnp.float32)
    first_slot = lax.axis_index("seq") * block_size
    slot_index = first_slot + jnp.arange(block_size, dtype=jnp.int32)
    active_slot = (slot_index[None, :] < cache_len[:, None])[:, None, None, None, :]
    causal = (jnp.arange(decode_count)[:, None] >= jnp.arange(decode_count)[None, :])[
        None, None, None
    ]
    old_scores = (
        jnp.einsum("rtkgd,rpkd->rkgtp", queries, cache_keys, preferred_element_type=jnp.float32)
        * score_scale
    )
    old_scores = jnp.where(active_slot, old_scores, NEG_FILL)
    old_top = jnp.max(old_scores, axis=-1)
    new_scores = (
        jnp.einsum("rtkgd,rukd->rkgtu", queries, keys_new, preferred_element_type=jnp.float32)
        * score_scale
    )
    new_scores = jnp.where(causal, new_scores, NEG_FILL)
    new_top = jnp.max(new_scores, axis=-1)
    row_top = lax.pmax(jnp.maximum(old_top, new_top), "seq")
    old_weights = jnp.where(active_slot, jnp.exp(old_scores - row_top[..., None]), 0.0)
    old_total, old_pooled = lax.psum(
        (
            jnp.sum(old_weights, axis=-1),
            jnp.einsum("rkgtp,rpkd->rkgtd", old_weights, cache_values, precision=highest),
        ),
        "seq",
    )
    new_weights = jnp.where(causal, jnp.exp(new_scores - row_top[..., None]), 0.0)
    denominator = old_total + jnp.sum(new_weights, axis=-1)
    pooled = old_pooled + jnp.einsum(
        "rkgtu,rukd->rkgtd", new_weights, values_new.astype(jnp.float32), precision=highest
    )
    attended = (
        (pooled / denominator[..., None])
        .transpose(0, 3, 1, 2, 4)
        .reshape(row_count, heads_here * HD)
        .astype(jnp.bfloat16)
    )
    return lax.psum_scatter(
        jnp.dot(attended, w_out, preferred_element_type=jnp.float32).astype(jnp.bfloat16),
        "mp",
        scatter_dimension=0,
        tiled=True,
    )


def solution(mesh):
    return jax.shard_map(
        shards,
        mesh=mesh,
        in_specs=(
            P("seq", None),
            P("seq", "mp"),
            P("seq", "mp"),
            P("seq", "mp"),
            P("mp", "seq"),
            P(None, None, "seq", "mp"),
            P(),
        ),
        out_specs=P("mp", "seq"),
        check_vma=False,
    )
```

profile of v0, /device:TPU:0, one launch (start us, length us, event | category | flops | bytes accessed | tf_op | source)
XLA Modules:
  0.0 416.0 jit_solution(5943476113532040646)
XLA Ops:
  6.5 1.1 fusion.21
  7.7 1.6 fusion.22
  9.3 8.3 %all-to-all-start = ((bf16[8,16,512]{2,0,1:T(8,128)(2,1)}), bf16[8,16,512]{2,0,1:T(8,128)(2,1)S(1)}, u32[]{:S(2)}, u32[]{:S(2)}) async-start(bf16[8,16,512]{2,0,1:T(8,128)(2,1)} %bitcast), calls=%async_computation | async-start | bytes 262144 | tf_op jit(solution)/shard_map/all_to_all | solution.py:40
  17.7 7.7 %all-to-all-done = bf16[8,16,512]{2,0,1:T(8,128)(2,1)S(1)} async-done(((bf16[8,16,512]{2,0,1:T(8,128)(2,1)}), bf16[8,16,512]{2,0,1:T(8,128)(2,1)S(1)}, u32[]{:S(2)}, u32[]{:S(2)}) %all-to-all-start) | async-done | bytes 131104 | tf_op jit(solution)/shard_map/all_to_all | solution.py:40
  25.4 2.9 convolution_bitcast_fusion
  28.4 1.7 copy.37
  30.2 0.7 copy.53
  31.0 11.8 %fusion.33 = (bf16[1,32,256,512]{3,2,1,0:T(8,128)(2,1)}, bf16[1,32,256,512]{3,2,1,0:T(8,128)(2,1)}) fusion(bf16[2,32,256,512]{3,2,1,0:T(8,128)(2,1)} %param.12), kind=kLoop, calls=%fused_computation.58 | loop fusion | bytes 33554432 | tf_op jit(solution)/shard_map/slice | solution.py:67
  42.8 12.0 %copy.35 = bf16[1,32,256,512]{2,3,1,0:T(8,128)(2,1)} copy(bf16[1,32,256,512]{3,2,1,0:T(8,128)(2,1)} %get-tuple-element.10) | data formatting | bytes 16777216
  54.8 11.9 %copy.34 = bf16[1,32,256,512]{2,3,1,0:T(8,128)(2,1)} copy(bf16[1,32,256,512]{3,2,1,0:T(8,128)(2,1)} %get-tuple-element.9) | data formatting | bytes 16777216
  67.4 92.3 %all-reduce.8.cloned.1.call-done = (f32[128,32,128]{2,1,0:T(8,128)}, f32[128,4,128]{2,0,1:T(8,128)}) async-done(((f32[128,32,128]{2,1,0:T(8,128)}, f32[128,4,128]{2,0,1:T(8,128)}), (f32[128,32,128]{2,1,0:T(8,128)}, f32[128,4,128]{2,0,1:T(8,128)})) %all-reduce.8.cloned.1.call-update) | async-done | bytes 2359312 | tf_op jit(solution)/shard_map/psum | solution.py:52
  159.6 3.1 subtract_convert_fusion
  162.9 7.1 %bitcast_reduce_fusion = (f32[32,4,8,4]{2,3,1,0:T(4,128)S(1)}, f32[32,4,4,8,256]{4,3,2,1,0:T(8,128)}) fusion(pred[32,256]{1,0:T(8,128)(4,1)S(1)} %broadcast_compare_fusion, bf16[32,256,4,128,1]{1,3,4,2,0:T(8,128)(2,1)} %bitcast.63, bf16[32,4,4,8,64]{4,3,2,1,0:T(8,128)(2,1)S(1)} %bitcast.67, bf16[32,4,4,8,64]{4,3,2,1,0:T(8,128)(2,1)S(1)} %bitcast.65), kind=kOutput, calls=%fused_computation.1 | convolution fusion | flops 273674240 | bytes 13656064 | tf_op jit(solution)/shard_map/rtkgd,rpkd->rkgtp/dot_general | solution.py:76
  170.0 5.0 %fusion.34 = (f32[32,4,8,4]{2,3,1,0:T(4,128)S(1)}, f32[32,4,8,4,4]{2,4,3,1,0:T(4,128)S(1)}) fusion(pred[4,4]{1,0:T(4,128)(4,1)S(1)} %iota_compare_fusion, bf16[32,4,4,64]{3,1,0,2:T(4,128)(2,1)S(1)} %bitcast.71, bf16[32,4,4,64]{3,1,0,2:T(4,128)(2,1)S(1)} %bitcast.70, bf16[32,4,4,8,64]{4,3,2,1,0:T(8,128)(2,1)S(1)} %bitcast.68, ...), kind=kOutput, calls=%fused_computation.59 | convolution fusion | flops 6598656 | bytes 1261584 | tf_op jit(solution)/shard_map/rtkgd,rukd->rkgtu/dot_general | solution.py:82
  175.1 78.2 %pmax.7 = f32[32,4,8,4]{2,3,1,0:T(4,128)S(1)} all-reduce(f32[32,4,8,4]{2,3,1,0:T(4,128)S(1)} %max.14), channel_id=1, replica_groups=mesh['seq'=16,'mp'=2] {'seq'}, use_global_device_ids=true, to_apply=%region_5.6 | all-reduce | flops 4096 | bytes 32768 | tf_op jit(solution)/shard_map/pmax | solution.py:87
  253.3 14.2 %fusion.3 = f32[32,4,8,4,128]{4,2,3,1,0:T(8,128)} fusion(bf16[32,256,4,128,1]{1,3,4,2,0:T(8,128)(2,1)} %bitcast.62, f32[32,4,4,8,256]{4,3,2,1,0:T(8,128)} %get-tuple-element.18, f32[32,4,8,4]{2,3,1,0:T(4,128)S(1)} %pmax.7, pred[32,256]{1,0:T(8,128)(4,1)S(1)} %broadcast_compare_fusion), kind=kOutput, calls=%fused_computation.6 | convolution fusion | flops 1614807040 | bytes 14704640 | tf_op jit(solution)/shard_map/rkgtp,rpkd->rkgtd/dot_general | solution.py:92
  267.8 3.6 fusion.2
  271.4 81.3 %all-reduce.9 = (f32[32,4,8,4]{2,3,1,0:T(4,128)S(1)}, bf16[128,512]{1,0:T(8,128)(2,1)S(1)}) all-reduce(f32[32,4,8,4]{2,3,1,0:T(4,128)S(1)} %fusion.2, f32[128,512]{1,0:T(8,128)S(1)} %fusion.25), channel_id=1, replica_groups=mesh['seq'=16,'mp'=2] {'seq'}, use_global_device_ids=true, to_apply=%region_9.10 | all-reduce | flops 69632 | bytes 425984 | tf_op jit(solution)/shard_map/psum | solution.py:89
  352.7 1.0 fusion.17
  353.8 40.5 %all-reduce.6.cloned.1.call-done = f32[32,4,8,4,128]{4,2,3,1,0:T(8,128)} async-done(((f32[32,4,8,4,128]{4,2,3,1,0:T(8,128)}), f32[32,4,8,4,128]{4,2,3,1,0:T(8,128)}) %all-reduce.6.cloned.1.call-update) | async-done | bytes 2097168 | tf_op jit(solution)/shard_map/psum | solution.py:89
  394.4 3.8 fusion.11
  398.4 0.5 convert_element_type.47
  398.9 3.5 convolution_convert_fusion
  402.5 7.0 %reduce-scatter.2.cloned.1.call-done = bf16[64,512]{1,0:T(8,128)(2,1)} async-done(((bf16[128,512]{1,0:T(8,128)(2,1)}), bf16[64,512]{1,0:T(8,128)(2,1)}) %reduce-scatter.2.cloned.1.call-update) | async-done | bytes 65552 | tf_op jit(solution)/shard_map/reduce_scatter | solution.py:107
  (31 shorter events, 1.8 us)
Async XLA Ops:
  6.5 23.5 %copy-start = (bf16[512,512]{1,0:T(8,128)(2,1)S(1)}, bf16[512,512]{1,0:T(8,128)(2,1)}, u32[]{:S(2)}) copy-start(bf16[512,512]{1,0:T(8,128)(2,1)} %param.9) | copy-start | bytes 1572868
  9.3 16.1 %all-to-all-start = ((bf16[8,16,512]{2,0,1:T(8,128)(2,1)}), bf16[8,16,512]{2,0,1:T(8,128)(2,1)S(1)}, u32[]{:S(2)}, u32[]{:S(2)}) async-start(bf16[8,16,512]{2,0,1:T(8,128)(2,1)} %bitcast), calls=%async_computation | async-start | bytes 262144 | tf_op jit(solution)/shard_map/all_to_all | solution.py:40
  17.6 142.0 %all-reduce.8.cloned.1.call-start = ((), (), s32[]{:S(2)}) async-start(), calls=%async_computation.4 | async-start | bytes 4718592 | tf_op jit(solution)/shard_map/psum | solution.py:52
  31.0 363.4 %all-reduce.6.cloned.1.call-start = ((), (), s32[]{:S(2)}) async-start(), calls=%async_computation.2 | async-start | bytes 4194304 | tf_op jit(solution)/shard_map/psum | solution.py:89
  54.8 11.9 %copy-start.4 = (s32[32]{0:T(128)S(1)}, s32[32]{0:T(128)}, u32[]{:S(2)}) copy-start(s32[32]{0:T(128)} %param.13) | copy-start | bytes 388
  159.6 3.1 copy-start.2
  253.3 14.3 %copy-start.3 = (bf16[512,512]{1,0:T(8,128)(2,1)S(1)}, bf16[512,512]{1,0:T(8,128)(2,1)}, u32[]{:S(2)}) copy-start(bf16[512,512]{1,0:T(8,128)(2,1)} %param.10) | copy-start | bytes 1572868
  267.5 142.0 %reduce-scatter.2.cloned.1.call-start = ((), (), s32[]{:S(2)}) async-start(), calls=%async_computation.3 | async-start | bytes 196608 | tf_op jit(solution)/shard_map/reduce_scatter | solution.py:107
  398.2 11.3 %copy-start.1 = (bf16[512,512]{1,0:T(8,128)(2,1)S(1)}, bf16[512,512]{1,0:T(8,128)(2,1)}, u32[]{:S(2)}) copy-start(bf16[512,512]{1,0:T(8,128)(2,1)} %param.9) | copy-start | bytes 1572868
Sparse Core Ops, SparseCore 0:
  31.1 128.4 all-reduce.7
  267.6 126.7 all-reduce.5
  402.6 6.8 reduce-scatter.1
where the time goes:
time: 417 us; the launch traced here: 416 us
  blocking collectives  159 us (38%)
  waiting for transfers between devices  148 us (35%)
  local copies, waits for them, and re-layouts  38.9 us (9%)
  matrix products  37.1 us (9%)
  between operations  13.3 us (3%)
  other arithmetic  11.3 us (3%)
  starting transfers between devices  8.44 us (2%)
    psum x1, waiting for transfers between devices, shards(): lax.psum((partial_query, partial_key, partial_value), 'seq')  92.3 us
    psum x1, blocking collectives, shards(): lax.psum((jnp.sum(old_weights, axis=-1), jnp.einsum('rkgtp,rpkd->rkgtd',...  81.3 us
    pmax x1, blocking collectives, shards(): row_top = lax.pmax(jnp.maximum(old_top, new_top), 'seq')  78.2 us
    psum x1, waiting for transfers between devices, shards(): lax.psum((jnp.sum(old_weights, axis=-1), jnp.einsum('rkgtp,rpkd->rkgtd',...  40.5 us
    unnamed x13, local copies, waits for them, and re-layouts  25.6 us
    dot_general x1, matrix products, shards(): jnp.einsum('rkgtp,rpkd->rkgtd', old_weights, cache_values, precision=high...  14.2 us
    slice x1, local copies, waits for them, and re-layouts, shards(): cache_keys = kv_cache[0].reshape(request_count, block_size, kv_here, HD)  11.8 us
  transfers between devices with their start and end apart: 4, of which 4 were waited for; matrix products, arithmetic and copies ran while one was open for 10% of the time, Pallas kernels for 0%

commit v1 on v0

--- a/solution.py
+++ b/solution.py
@@ -1,8 +1,11 @@
+import functools
 import math
 
 import jax
 import jax.numpy as jnp
 from jax import lax
+from jax.experimental import pallas as pl
+from jax.experimental.pallas import tpu as pltpu
 from jax.sharding import PartitionSpec as P
 
 HD = 128
@@ -112,9 +115,410 @@
     )
 
 
+def fused_kernel(
+    n, steps, scale, cos_ref, sin_ref, len_ref, x_ref, wq_hbm, wk_hbm, wv_hbm, wo_hbm, kv_hbm,
+    out_ref,
+    wq, wk, wv, wo, kv, nsend, xrecv, psend, prec, zsend, zrecv, acc, qall, knew, vnew,
+    osend, lsend, orecv, lrecv, accf, attg, pf, msend, mrecv,
+    w_sem, kv_sem, s_x, r_x, s_o, r_o, s_l, r_l, s_q, r_q, s_a, r_a, s_p, r_p, s_z, r_z, m_sem,
+):
+    me = lax.axis_index("seq")
+    core = lax.axis_index("mp")
+    f32, bf16 = jnp.float32, jnp.bfloat16
+    rp, width = x_ref.shape
+    depth = width // n
+    rows = n * rp
+    heads = wq.shape[1] // HD
+    kvh = wk.shape[1] // HD
+    group = heads // kvh
+    per = rp // steps
+    block = kv.shape[2]
+    qcols = heads * HD
+    kcols = kvh * HD
+
+    weights = [
+        pltpu.make_async_copy(wq_hbm, wq, w_sem.at[0]),
+        pltpu.make_async_copy(wk_hbm, wk, w_sem.at[1]),
+        pltpu.make_async_copy(wv_hbm, wv, w_sem.at[2]),
+    ]
+    out_weight = pltpu.make_async_copy(wo_hbm, wo, w_sem.at[3])
+
+    def cache_copy(j):
+        at = (slice(None), pl.ds(j * per, per))
+        return pltpu.make_async_copy(kv_hbm.at[at], kv.at[at], kv_sem.at[j])
+
+    for copy in weights:
+        copy.start()
+
+    barrier = pltpu.get_barrier_semaphore()
+
+    def greet(d, _):
+        pl.semaphore_signal(barrier, inc=1, device_id={"seq": lax.rem(me + d, n)},
+                            device_id_type=pl.DeviceIdType.MESH)
+        return _
+
+    lax.fori_loop(1, n, greet, 0)
+    pl.semaphore_signal(barrier, inc=1, device_id={"mp": 1 - core},
+                        device_id_type=pl.DeviceIdType.MESH)
+
+    def remote(src, dst, send, recv, d):
+        return pltpu.make_async_remote_copy(
+            src_ref=src, dst_ref=dst, send_sem=send.at[d], recv_sem=recv.at[d],
+            device_id={"seq": lax.rem(me + d, n)}, device_id_type=pl.DeviceIdType.MESH)
+
+    def x_copy(d):
+        return remote(nsend.at[lax.rem(me + d, n)], xrecv.at[me], s_x, r_x, d)
+
+    def o_copy(j, slot):
+        return pltpu.make_async_remote_copy(
+            src_ref=osend.at[j], dst_ref=orecv.at[slot], send_sem=s_o.at[j], recv_sem=r_o.at[slot],
+            device_id={"seq": j}, device_id_type=pl.DeviceIdType.MESH)
+
+    def l_copy(j, slot):
+        return pltpu.make_async_remote_copy(
+            src_ref=lsend.at[j], dst_ref=lrecv.at[slot], send_sem=s_l.at[j], recv_sem=r_l.at[slot],
+            device_id={"seq": j}, device_id_type=pl.DeviceIdType.MESH)
+
+    deep = n // 4
+    x_at, y_at, z_at = lax.rem(me, 2), lax.rem(lax.div(me, 2), 2), lax.div(me, 4)
+    x_peer = me + 1 - 2 * x_at
+    y_peer = me + 2 - 4 * y_at
+
+    def source(kind, dz):
+        z = lax.rem(z_at - dz + deep, deep)
+        x = x_at + lax.rem(kind, 2) * (1 - 2 * x_at)
+        y = y_at + lax.div(kind, 2) * (1 - 2 * y_at)
+        return z * 4 + y * 2 + x
+
+    def p_copy(dz, kind):
+        return pltpu.make_async_remote_copy(
+            src_ref=psend.at[source(kind, deep - dz)], dst_ref=prec.at[dz, kind - 1],
+            send_sem=s_p.at[dz, kind], recv_sem=r_p.at[dz, kind],
+            device_id={"seq": source(kind, 0)}, device_id_type=pl.DeviceIdType.MESH)
+
+    def z_copy(dz):
+        return remote(zsend.at[dz], zrecv.at[dz], s_z, r_z, 4 * dz)
+
+    class Gather:
+        def __init__(self, ref, low, high, send, recv):
+            self.ref, self.low, self.high, self.send, self.recv = ref, low, high, send, recv
+
+        def copy(self, view, way, dz, target):
+            return pltpu.make_async_remote_copy(
+                src_ref=view, dst_ref=view, send_sem=self.send.at[way, dz],
+                recv_sem=self.recv.at[way, dz],
+                device_id={"seq": target}, device_id_type=pl.DeviceIdType.MESH)
+
+        def z(self, dz):
+            return self.copy(self.ref.at[me], 0, dz, lax.rem(me + 4 * dz, n))
+
+        def x(self, dz):
+            return self.copy(self.ref.at[source(0, dz)], 1, dz, x_peer)
+
+        def y(self, dz):
+            return self.copy(self.ref.at[source(0, dz)], 2, dz, y_peer)
+
+        def xy(self, dz):
+            return self.copy(self.low(self.ref, source(1, dz)), 3, dz, y_peer)
+
+        def yx(self, dz):
+            return self.copy(self.high(self.ref, source(2, dz)), 4, dz, x_peer)
+
+        def begin(self):
+            each(lambda dz: self.z(dz).start(), 1, deep)
+            self.x(0).start()
+            self.y(0).start()
+
+        def spread(self, dz):
+            self.z(dz).wait_recv()
+            self.x(dz).start()
+            self.y(dz).start()
+
+        def forward(self, dz):
+            self.x(dz).wait_recv()
+            self.xy(dz).start()
+            self.y(dz).wait_recv()
+            self.yx(dz).start()
+
+        def finish(self, dz):
+            self.xy(dz).wait_recv()
+            self.yx(dz).wait_recv()
+
+        def sent(self, dz):
+            self.x(dz).wait_send()
+            self.y(dz).wait_send()
+            self.xy(dz).wait_send()
+            self.yx(dz).wait_send()
+
+        def drain(self):
+            each(lambda dz: self.z(dz).wait_send(), 1, deep)
+            each(self.sent, 0, deep)
+
+    def each(action, first=1, last=n):
+        def body(d, _):
+            action(d)
+            return _
+        lax.fori_loop(first, last, body, 0)
+
+    some = heads // 2
+    queries = Gather(qall, lambda ref, j: ref.at[j, 0:some], lambda ref, j: ref.at[j, some:heads],
+                     s_q, r_q)
+    results = Gather(attg, lambda ref, j: ref.at[j, :, 0:some * HD],
+                     lambda ref, j: ref.at[j, :, some * HD:qcols], s_a, r_a)
+
+    widened = x_ref[...].astype(f32)
+    norm = widened * lax.rsqrt(jnp.mean(widened * widened, axis=-1, keepdims=True) + 1e-05)
+    for j in range(n):
+        nsend[j] = norm[:, j * depth:(j + 1) * depth].astype(bf16)
+    xrecv[me] = nsend[me]
+    pl.semaphore_wait(barrier, n)
+    each(lambda d: x_copy(d).start())
+    each(lambda d: cache_copy(d).start(), 0)
+    out_weight.start()
+    for copy in weights:
+        copy.wait()
+    each(lambda d: x_copy(d).wait_recv())
+
+    gathered = xrecv[...].astype(f32).reshape(rows, depth).astype(bf16)
+
+    def project(weight, count, first):
+        tile = min(512, count)
+        for c in range(count // tile):
+            part = jnp.dot(gathered, weight[:, c * tile:(c + 1) * tile], preferred_element_type=f32)
+            psend[:, :, first + c * tile:first + (c + 1) * tile] = part.reshape(
+                n, rp, tile).astype(bf16)
+
+    project(wq, qcols, 0)
+    project(wk, kcols, qcols)
+    project(wv, kcols, qcols + kcols)
+
+    def release(dz):
+        for kind in (3, 1, 2):
+            p_copy(dz, kind).start()
+
+    def plane_sum(dz):
+        total = psend[source(0, deep - dz)].astype(f32)
+        for kind in (3, 1, 2):
+            p_copy(dz, kind).wait_recv()
+        for kind in (3, 1, 2):
+            total += prec[dz, kind - 1].astype(f32)
+        return total
+
+    def pass_on(dz):
+        zsend[dz] = plane_sum(dz)
+        z_copy(dz).start()
+
+    def add(dz):
+        z_copy(dz).wait_recv()
+        acc[...] += zrecv[dz]
+
+    each(release, 1, deep)
+    release(0)
+    each(pass_on, 1, deep)
+    acc[...] = plane_sum(0)
+    each(add, 1, deep)
+
+    cosine = cos_ref[...]
+    sines = sin_ref[...]
+
+    def turn(column):
+        value = acc[:, column:column + HD]
+        return value * cosine + pltpu.roll(value, HD // 2, 1) * sines
+
+    for h in range(heads):
+        qall[me, h] = turn(h * HD).astype(bf16)
+    queries.begin()
+    for k in range(kvh):
+        knew[k] = jnp.zeros(knew.shape[1:], bf16)
+        vnew[k] = jnp.zeros(vnew.shape[1:], bf16)
+        knew[k, 0:rp] = turn(qcols + k * HD).astype(bf16)
+        column = qcols + kcols + k * HD
+        vnew[k, 0:rp] = acc[:, column:column + HD].astype(bf16)
+
+    lane = lax.broadcasted_iota(jnp.int32, (rp, HD), 1)
+    m_rows = group * rp
+
+    def attend(query, keys, values, bias, o_ref, l_ref, at):
+        stats = jnp.zeros((rp, HD), f32)
+        for k in range(kvh):
+            q = query(k).astype(f32).reshape(m_rows, HD).astype(bf16)
+            scores = lax.dot_general(q, keys(k), (((1,), (1,)), ((), ())),
+                                     preferred_element_type=f32) * scale + bias
+            top = jnp.max(scores, axis=-1, keepdims=True)
+            weight = jnp.exp(scores - top)
+            total = jnp.sum(weight, axis=-1, keepdims=True)
+            pooled = jnp.dot(weight.astype(bf16), values(k), preferred_element_type=f32)
+            pooled = pooled * (1.0 / total)
+            o_ref[at, k * group:(k + 1) * group] = pooled.reshape(group, rp, HD).astype(bf16)
+            level = top + jnp.log(total)
+            for g in range(group):
+                stats = jnp.where(lane == k * group + g, level[g * rp:(g + 1) * rp], stats)
+        l_ref[at] = stats
+
+    new = knew.shape[1]
+    row = lax.rem(lax.broadcasted_iota(jnp.int32, (m_rows, new), 0), rp)
+    col = lax.broadcasted_iota(jnp.int32, (m_rows, new), 1)
+    seen = (col <= row) & (lax.div(col, steps) == lax.div(row, steps))
+    attend(lambda k: qall[me, k * group:(k + 1) * group], lambda k: knew[k], lambda k: vnew[k],
+           jnp.where(seen, 0.0, NEG_FILL), orecv, lrecv, n)
+
+    span = per * block
+    row_request = lax.div(lax.rem(lax.broadcasted_iota(jnp.int32, (m_rows, span), 0), rp), steps)
+    slot = lax.broadcasted_iota(jnp.int32, (m_rows, span), 1)
+
+    def cached(j, o_ref, l_ref):
+        cache_copy(j).wait()
+        bias = jnp.full((m_rows, span), NEG_FILL, f32)
+        for r in range(per):
+            left = len_ref[j * per + r] - me * block
+            live = (row_request == r) & (slot >= r * block) & (slot < r * block + jnp.minimum(left, block))
+            bias = jnp.where(live, 0.0, bias)
+        here = pl.ds(j * per, per)
+        attend(lambda k: qall[j, k * group:(k + 1) * group],
+               lambda k: kv[0, here, :, k * HD:(k + 1) * HD].reshape(span, HD),
+               lambda k: kv[1, here, :, k * HD:(k + 1) * HD].reshape(span, HD),
+               bias, o_ref, l_ref, j)
+
+    def answer(j):
+        cached(j, osend, lsend)
+        o_copy(j, me).start()
+        l_copy(j, me).start()
+
+    queries.forward(0)
+    cached(me, orecv, lrecv)
+    each(queries.spread, 1, deep)
+
+    def own_line(dz):
+        answer(source(0, dz))
+        queries.forward(dz)
+
+    each(own_line, 1, deep)
+    each(lambda i: answer(source(1 + lax.div(i, deep), lax.rem(i, deep))), 0, 2 * deep)
+
+    def diagonal(dz):
+        queries.finish(dz)
+        answer(source(3, dz))
+
+    each(diagonal, 0, deep)
+
+    def arrived(d):
+        j = lax.rem(me + d, n)
+        o_copy(j, j).wait_recv()
+        l_copy(j, j).wait_recv()
+
+    each(arrived)
+
+    levels = lrecv[...]
+    top = jnp.max(levels, axis=0)
+    share = jnp.exp(levels - top[None])
+    lrecv[...] = share / jnp.sum(share, axis=0)[None]
+    accf[...] = jnp.zeros_like(accf)
+
+    def merge(s, _):
+        share_s = lrecv[s]
+        for h in range(heads):
+            accf[h] += share_s[:, h:h + 1] * orecv[s, h].astype(f32)
+        return _
+
+    lax.fori_loop(0, n + 1, merge, 0)
+    for h in range(heads):
+        attg[me, :, h * HD:(h + 1) * HD] = accf[h].astype(bf16)
+    results.begin()
+    results.forward(0)
+    each(results.spread, 1, deep)
+    each(results.forward, 1, deep)
+    out_weight.wait()
+    each(results.finish, 0, deep)
+
+    half = rows // 2
+    attended = attg[...].astype(f32).reshape(rows, qcols).astype(bf16)
+    part = jnp.dot(attended, wo[...], preferred_element_type=f32)
+    pf[...] = part.reshape(2, half, part.shape[1])
+    msend[...] = pf[1 - core].astype(bf16)
+    swap = pltpu.make_async_remote_copy(
+        src_ref=msend, dst_ref=mrecv, send_sem=m_sem.at[0], recv_sem=m_sem.at[1],
+        device_id={"mp": 1 - core}, device_id_type=pl.DeviceIdType.MESH)
+    swap.start()
+
+    def sent(d):
+        x_copy(d).wait_send()
+        j = lax.rem(me + d, n)
+        o_copy(j, me).wait_send()
+        l_copy(j, me).wait_send()
+
+    each(sent)
+
+    def summed(dz):
+        for kind in (1, 2, 3):
+            p_copy(dz, kind).wait_send()
+
+    each(summed, 0, deep)
+    each(lambda dz: z_copy(dz).wait_send(), 1, deep)
+    queries.drain()
+    results.drain()
+    swap.wait()
+    out_ref[...] = (pf[core] + mrecv[...].astype(f32)).astype(bf16)
+
+
+def fused(n, layer_input, w_query, w_key, w_value, w_out, kv_cache, cache_len):
+    rp = layer_input.shape[0]
+    rows = rp * n
+    depth = w_query.shape[0]
+    steps = rows // cache_len.shape[0]
+    heads = w_query.shape[1] // HD
+    kvh = w_key.shape[1] // HD
+    total = w_query.shape[1] + w_key.shape[1] + w_value.shape[1]
+    per = rp // steps
+    me = lax.axis_index("seq")
+    lengths = lax.dynamic_slice_in_dim(cache_len, me * per, per, 0)
+    positions = (lengths[:, None] + jnp.arange(steps, dtype=jnp.int32)[None, :]).reshape(rp)
+    angles = positions.astype(jnp.float32)[:, None] * inverse_freq()
+    cosine = jnp.cos(angles)
+    sines = jnp.sin(angles)
+    cosine = jnp.concatenate([cosine, cosine], axis=-1)
+    sines = jnp.concatenate([-sines, sines], axis=-1)
+    f32, bf16 = jnp.float32, jnp.bfloat16
+    vm = pltpu.VMEM
+    dma = pltpu.SemaphoreType.DMA
+    vmem = pl.BlockSpec(memory_space=pltpu.VMEM)
+    hbm = pl.BlockSpec(memory_space=pl.ANY)
+    cols = w_out.shape[1]
+    return pl.pallas_call(
+        functools.partial(fused_kernel, n, steps, 1.0 / math.sqrt(HD)),
+        out_shape=jax.ShapeDtypeStruct((rows // 2, cols), bf16),
+        in_specs=[vmem, vmem, pl.BlockSpec(memory_space=pltpu.SMEM), vmem] + [hbm] * 5,
+        out_specs=vmem,
+        scratch_shapes=[
+            vm(w_query.shape, bf16), vm(w_key.shape, bf16), vm(w_value.shape, bf16),
+            vm(w_out.shape, bf16), vm(kv_cache.shape, bf16),
+            vm((n, rp, depth), bf16), vm((n, rp, depth), bf16),
+            vm((n, rp, total), bf16), vm((n // 4, 3, rp, total), bf16),
+            vm((n // 4, rp, total), f32), vm((n // 4, rp, total), f32), vm((rp, total), f32),
+            vm((n, heads, rp, HD), bf16), vm((kvh, HD, HD), bf16), vm((kvh, HD, HD), bf16),
+            vm((n, heads, rp, HD), bf16), vm((n, rp, HD), f32),
+            vm((n + 1, heads, rp, HD), bf16), vm((n + 1, rp, HD), f32),
+            vm((heads, rp, HD), f32), vm((n, rp, heads * HD), bf16),
+            vm((2, rows // 2, cols), f32), vm((rows // 2, cols), bf16), vm((rows // 2, cols), bf16),
+            dma((4,)), dma((n,)),
+        ] + [dma((n,))] * 6 + [dma((5, n // 4))] * 4 + [dma((n // 4, 4))] * 2 + [dma((n,))] * 2 + [dma((2,))],
+        compiler_params=pltpu.CompilerParams(
+            collective_id=0, has_side_effects=True, vmem_limit_bytes=56 * 1024 * 1024),
+        name="decode_block",
+    )(cosine, sines, cache_len, layer_input, w_query, w_key, w_value, w_out, kv_cache)
+
+
+def block(n, mp, layer_input, w_query, w_key, w_value, w_out, kv_cache, cache_len):
+    rp = layer_input.shape[0]
+    steps = rp * n // cache_len.shape[0]
+    heads = w_query.shape[1] // HD
+    if mp == 2 and n == 16 and rp == 8 and rp % steps == 0 and heads <= HD:
+        return fused(n, layer_input, w_query, w_key, w_value, w_out, kv_cache, cache_len)
+    return shards(layer_input, w_query, w_key, w_value, w_out, kv_cache, cache_len)
+
+
 def solution(mesh):
     return jax.shard_map(
-        shards,
+        functools.partial(block, mesh.shape["seq"], mesh.shape["mp"]),
         mesh=mesh,
         in_specs=(
             P("seq", None),

time: 417 us -> 91.2 us (0.22)
  blocking collectives: 159 us -> 0 us
  waiting for transfers between devices: 148 us -> 0 us
  Pallas kernels: 0 us -> 87.8 us
  matrix products: 37.1 us -> 0 us
  local copies, waits for them, and re-layouts: 38.9 us -> 2.29 us
  between operations: 13.3 us -> 0.02 us
  other arithmetic: 11.3 us -> 0.88 us
  starting transfers between devices: 8.44 us -> 0 us
    psum x2 -> x0, waiting for transfers between devices: 133 us -> none  [the longest x1 92.3 us: shards(): lax.psum((partial_query, partial_key, partial_value), 'seq')]
    pallas_call x0 -> x1, Pallas kernels: none -> 87.8 us  [fused(): pl.pallas_call(functools.partial(fused_kernel, n, steps, 1.0 / math.sqrt(...]
    psum x1 -> x0, blocking collectives: 81.3 us -> none  [shards(): lax.psum((jnp.sum(old_weights, axis=-1), jnp.einsum('rkgtp,rpkd->rkgtd',...]
    pmax x1 -> x0, blocking collectives: 78.2 us -> none  [shards(): row_top = lax.pmax(jnp.maximum(old_top, new_top), 'seq')]
    dot_general x8 -> x0, matrix products: 37.1 us -> none  [the longest x1 14.2 us: shards(): jnp.einsum('rkgtp,rpkd->rkgtd', old_weights, cache_values, precision=high...]
    unnamed x13 -> x1, local copies, waits for them, and re-layouts: 25.6 us -> 1.47 us
    slice x1 -> x0, local copies, waits for them, and re-layouts: 11.8 us -> none  [shards(): cache_keys = kv_cache[0].reshape(request_count, block_size, kv_here, HD)]
    all_to_all x1 -> x0, starting transfers between devices: 8.31 us -> none  [shards(): lax.all_to_all(normed, 'seq', split_axis=1, concat_axis=0, tiled=True)]
  transfers between devices with their start and end apart: 4 -> 0, of which waited for: 4 -> 0; matrix products, arithmetic and copies ran while one was open for 10% -> 0% of each run, Pallas kernels for 0% -> 0%
where the time goes in v1:
time: 91.2 us; the launch traced here: 91 us
  Pallas kernels  87.8 us (96%)
  local copies, waits for them, and re-layouts  2.29 us (3%)
    pallas_call x1, Pallas kernels, fused(): pl.pallas_call(functools.partial(fused_kernel, n, steps, 1.0 / math.sqrt(...  87.8 us

profile of v1, /device:TPU:0, one launch (start us, length us, event | category | flops | bytes accessed | tf_op | source)
XLA Modules:
  0.0 91.0 jit_solution(9109442956175128053)
XLA Ops:
  0.0 0.7 dynamic_slice.3
  0.7 0.1 add_convert_fusion
  0.8 0.1 convert_element_type.11
  0.9 0.1 fusion
  1.0 0.7 pad_maximum_fusion
  1.7 87.8 %decode_block.1 = bf16[64,512]{1,0:T(8,128)(2,1)} custom-call(f32[8,128]{1,0:T(8,128)} %get-tuple-element.8.cos_ref, f32[8,128]{1,0:T(8,128)} %get-tuple-element.9.sin_ref, s32[32]{0:T(128)} %len_ref.1, bf16[8,8192]{1,0:T(8,128)(2,1)} %x_ref.1, bf16[512,4096]{1,0:T(8,128)(2,1)} %wq_hbm.1, bf16[512,512]{1,0:T(8,128)(2,1)} %wk_hbm.1, bf16[512,512]{1,0:T(8,128)(2,1)} %wv_hbm.1, ...), custom_call_target="tpu_custom_call" | custom-call | tf_op jit(solution)/shard_map/decode_block/pallas_call | solution.py:486
  89.5 1.5 %copy.9 = bf16[64,512]{1,0:T(8,128)(2,1)} copy(bf16[64,512]{1,0:T(8,128)(2,1)} %decode_block.1) | data formatting | bytes 131072
  (1 shorter events, 0.0 us)

commit v2 on v1

--- a/solution.py
+++ b/solution.py
@@ -200,29 +200,32 @@
         return remote(zsend.at[dz], zrecv.at[dz], s_z, r_z, 4 * dz)
 
     class Gather:
-        def __init__(self, ref, low, high, send, recv):
-            self.ref, self.low, self.high, self.send, self.recv = ref, low, high, send, recv
+        def __init__(self, view, part, send, recv):
+            self.whole = lambda j: view(j, 2 * part, 2 * part + 2)
+            self.low = lambda j: view(j, 2 * part, 2 * part + 1)
+            self.high = lambda j: view(j, 2 * part + 1, 2 * part + 2)
+            self.part, self.send, self.recv = part, send, recv
 
         def copy(self, view, way, dz, target):
             return pltpu.make_async_remote_copy(
-                src_ref=view, dst_ref=view, send_sem=self.send.at[way, dz],
-                recv_sem=self.recv.at[way, dz],
+                src_ref=view, dst_ref=view, send_sem=self.send.at[self.part, way, dz],
+                recv_sem=self.recv.at[self.part, way, dz],
                 device_id={"seq": target}, device_id_type=pl.DeviceIdType.MESH)
 
         def z(self, dz):
-            return self.copy(self.ref.at[me], 0, dz, lax.rem(me + 4 * dz, n))
+            return self.copy(self.whole(me), 0, dz, lax.rem(me + 4 * dz, n))
 
         def x(self, dz):
-            return self.copy(self.ref.at[source(0, dz)], 1, dz, x_peer)
+            return self.copy(self.whole(source(0, dz)), 1, dz, x_peer)
 
         def y(self, dz):
-            return self.copy(self.ref.at[source(0, dz)], 2, dz, y_peer)
+            return self.copy(self.whole(source(0, dz)), 2, dz, y_peer)
 
         def xy(self, dz):
-            return self.copy(self.low(self.ref, source(1, dz)), 3, dz, y_peer)
+            return self.copy(self.low(source(1, dz)), 3, dz, y_peer)
 
         def yx(self, dz):
-            return self.copy(self.high(self.ref, source(2, dz)), 4, dz, x_peer)
+            return self.copy(self.high(source(2, dz)), 4, dz, x_peer)
 
         def begin(self):
             each(lambda dz: self.z(dz).start(), 1, deep)
@@ -260,11 +263,11 @@
             return _
         lax.fori_loop(first, last, body, 0)
 
-    some = heads // 2
-    queries = Gather(qall, lambda ref, j: ref.at[j, 0:some], lambda ref, j: ref.at[j, some:heads],
-                     s_q, r_q)
-    results = Gather(attg, lambda ref, j: ref.at[j, :, 0:some * HD],
-                     lambda ref, j: ref.at[j, :, some * HD:qcols], s_a, r_a)
+    hq, cq = heads // 4, qcols // 4
+    queries = [Gather(lambda j, a, b: qall.at[j, a * hq:b * hq], part, s_q, r_q)
+               for part in range(2)]
+    results = [Gather(lambda j, a, b: attg.at[j, :, a * cq:b * cq], part, s_a, r_a)
+               for part in range(2)]
 
     widened = x_ref[...].astype(f32)
     norm = widened * lax.rsqrt(jnp.mean(widened * widened, axis=-1, keepdims=True) + 1e-05)
@@ -325,9 +328,10 @@
         value = acc[:, column:column + HD]
         return value * cosine + pltpu.roll(value, HD // 2, 1) * sines
 
-    for h in range(heads):
-        qall[me, h] = turn(h * HD).astype(bf16)
-    queries.begin()
+    for part in range(2):
+        for h in range(part * heads // 2, (part + 1) * heads // 2):
+            qall[me, h] = turn(h * HD).astype(bf16)
+        queries[part].begin()
     for k in range(kvh):
         knew[k] = jnp.zeros(knew.shape[1:], bf16)
         vnew[k] = jnp.zeros(vnew.shape[1:], bf16)
@@ -384,19 +388,23 @@
         o_copy(j, me).start()
         l_copy(j, me).start()
 
-    queries.forward(0)
+    queries[0].forward(0)
+    queries[1].forward(0)
     cached(me, orecv, lrecv)
-    each(queries.spread, 1, deep)
+    each(queries[0].spread, 1, deep)
+    each(queries[1].spread, 1, deep)
 
     def own_line(dz):
         answer(source(0, dz))
-        queries.forward(dz)
+        queries[0].forward(dz)
+        queries[1].forward(dz)
 
     each(own_line, 1, deep)
     each(lambda i: answer(source(1 + lax.div(i, deep), lax.rem(i, deep))), 0, 2 * deep)
 
     def diagonal(dz):
-        queries.finish(dz)
+        queries[0].finish(dz)
+        queries[1].finish(dz)
         answer(source(3, dz))
 
     each(diagonal, 0, deep)
@@ -414,26 +422,38 @@
     lrecv[...] = share / jnp.sum(share, axis=0)[None]
     accf[...] = jnp.zeros_like(accf)
 
-    def merge(s, _):
-        share_s = lrecv[s]
-        for h in range(heads):
-            accf[h] += share_s[:, h:h + 1] * orecv[s, h].astype(f32)
-        return _
-
-    lax.fori_loop(0, n + 1, merge, 0)
-    for h in range(heads):
-        attg[me, :, h * HD:(h + 1) * HD] = accf[h].astype(bf16)
-    results.begin()
-    results.forward(0)
-    each(results.spread, 1, deep)
-    each(results.forward, 1, deep)
+    for part in range(2):
+        mine = range(part * heads // 2, (part + 1) * heads // 2)
+
+        def merge(s, _):
+            share_s = lrecv[s]
+            for h in mine:
+                accf[h] += share_s[:, h:h + 1] * orecv[s, h].astype(f32)
+            return _
+
+        lax.fori_loop(0, n + 1, merge, 0)
+        for h in mine:
+            attg[me, :, h * HD:(h + 1) * HD] = accf[h].astype(bf16)
+        results[part].begin()
+    for part in range(2):
+        results[part].forward(0)
+        each(results[part].spread, 1, deep)
+    for part in range(2):
+        each(results[part].forward, 1, deep)
     out_weight.wait()
-    each(results.finish, 0, deep)
 
     half = rows // 2
-    attended = attg[...].astype(f32).reshape(rows, qcols).astype(bf16)
-    part = jnp.dot(attended, wo[...], preferred_element_type=f32)
-    pf[...] = part.reshape(2, half, part.shape[1])
+    part_cols = qcols // 2
+    for part in range(2):
+        each(results[part].finish, 0, deep)
+        at = slice(part * part_cols, (part + 1) * part_cols)
+        attended = attg[:, :, at].astype(f32).reshape(rows, part_cols).astype(bf16)
+        product = jnp.dot(attended, wo[at], preferred_element_type=f32)
+        product = product.reshape(2, half, product.shape[1])
+        if part == 0:
+            pf[...] = product
+        else:
+            pf[...] += product
     msend[...] = pf[1 - core].astype(bf16)
     swap = pltpu.make_async_remote_copy(
         src_ref=msend, dst_ref=mrecv, send_sem=m_sem.at[0], recv_sem=m_sem.at[1],
@@ -454,8 +474,8 @@
 
     each(summed, 0, deep)
     each(lambda dz: z_copy(dz).wait_send(), 1, deep)
-    queries.drain()
-    results.drain()
+    for gather in queries + results:
+        gather.drain()
     swap.wait()
     out_ref[...] = (pf[core] + mrecv[...].astype(f32)).astype(bf16)
 
@@ -500,7 +520,7 @@
             vm((heads, rp, HD), f32), vm((n, rp, heads * HD), bf16),
             vm((2, rows // 2, cols), f32), vm((rows // 2, cols), bf16), vm((rows // 2, cols), bf16),
             dma((4,)), dma((n,)),
-        ] + [dma((n,))] * 6 + [dma((5, n // 4))] * 4 + [dma((n // 4, 4))] * 2 + [dma((n,))] * 2 + [dma((2,))],
+        ] + [dma((n,))] * 6 + [dma((2, 5, n // 4))] * 4 + [dma((n // 4, 4))] * 2 + [dma((n,))] * 2 + [dma((2,))],
         compiler_params=pltpu.CompilerParams(
             collective_id=0, has_side_effects=True, vmem_limit_bytes=56 * 1024 * 1024),
         name="decode_block",
@@ -511,7 +531,7 @@
     rp = layer_input.shape[0]
     steps = rp * n // cache_len.shape[0]
     heads = w_query.shape[1] // HD
-    if mp == 2 and n == 16 and rp == 8 and rp % steps == 0 and heads <= HD:
+    if mp == 2 and n == 16 and rp == 8 and rp % steps == 0 and heads <= HD and heads % 4 == 0:
         return fused(n, layer_input, w_query, w_key, w_value, w_out, kv_cache, cache_len)
     return shards(layer_input, w_query, w_key, w_value, w_out, kv_cache, cache_len)
 

time: 91.2 us -> 91.8 us (level)
  no operation moved by 1% of the time
where the time goes in v2:
time: 91.8 us; the launch traced here: 91.6 us
  Pallas kernels  88.4 us (96%)
  local copies, waits for them, and re-layouts  2.29 us (2%)
    pallas_call x1, Pallas kernels, fused(): pl.pallas_call(functools.partial(fused_kernel, n, steps, 1.0 / math.sqrt(...  88.4 us

profile of v2, /device:TPU:0, one launch (start us, length us, event | category | flops | bytes accessed | tf_op | source)
XLA Modules:
  0.0 91.6 jit_solution(16476884885687519808)
XLA Ops:
  0.0 0.7 dynamic_slice.3
  0.7 0.1 add_convert_fusion
  0.8 0.1 convert_element_type.11
  0.9 0.1 fusion
  1.0 0.7 pad_maximum_fusion
  1.7 88.4 %decode_block.1 = bf16[64,512]{1,0:T(8,128)(2,1)} custom-call(f32[8,128]{1,0:T(8,128)} %get-tuple-element.8.cos_ref, f32[8,128]{1,0:T(8,128)} %get-tuple-element.9.sin_ref, s32[32]{0:T(128)} %len_ref.1, bf16[8,8192]{1,0:T(8,128)(2,1)} %x_ref.1, bf16[512,4096]{1,0:T(8,128)(2,1)} %wq_hbm.1, bf16[512,512]{1,0:T(8,128)(2,1)} %wk_hbm.1, bf16[512,512]{1,0:T(8,128)(2,1)} %wv_hbm.1, ...), custom_call_target="tpu_custom_call" | custom-call | tf_op jit(solution)/shard_map/decode_block/pallas_call | solution.py:506
  90.1 1.5 %copy.9 = bf16[64,512]{1,0:T(8,128)(2,1)} copy(bf16[64,512]{1,0:T(8,128)(2,1)} %decode_block.1) | data formatting | bytes 131072
  (1 shorter events, 0.0 us)
